TPU v7x, 256 devices: a whole 4x4x8 slice. The times are simulated.
256 devices in a mesh: tm: 128 (over z, y, x), rows: 2 (over core).
Axes of the slice: x: 4, y: 4, z: 8, core: 2. Of those that a mesh axis runs over, the one named last changes fastest.
Arguments:
- site_rates: float32 [256], replicated, may hold values from 0.0005 to 0.2
- prior_mean: float32 [512, 384], replicated, may hold values from -6 to 6
- observed: float32 [128, 256, 384], P('tm'), may hold values from -6 to 6
- obs_mask: int32 [128, 256], P('tm'), may hold values 0 or 1
- filter_gains: float32 [128, 512, 256], P('tm', 'rows'), may hold values from -0.05 to 0.8, as said below
- smooth_gains: float32 [128, 512, 512], P('tm', 'rows'), may hold values from -0.02 to 1, as said below
Outputs:
- filtered: float32 [128, 512, 384], P('tm', 'rows')
- smoothed: float32 [128, 512, 384], P('tm', 'rows')
Inputs may be any that keep to these rules, and one draw needn't show every extreme that they name: `filter_gains`: gain of each step; row 2i + c is component c of site i, column j a site. `smooth_gains`: smoother gain of each step; rows and columns are state entries.
All inputs are finite; a program needn't handle non-finite values. No bound on the sum of `obs_mask` on one device may be relied on, other than what follows from the above.
Results may differ from a plain program's by a relative error of at most 0.0003.
Values sent between devices are 32-bit elements; how exact they have to be, the bound alone decides.
A program may use at most 128 MiB of HBM per device.

v0:
```python
import jax
import jax.numpy as jnp
from jax import lax
from jax.sharding import PartitionSpec as P


def shifted(value, axis, steps):
    count = lax.axis_size(axis)
    first, last = (max(0, -steps), min(count, count - steps))
    return lax.ppermute(value, axis, [(source, source + steps) for source in range(first, last)])


def product(left, right):
    return jnp.dot(left, right, precision=lax.Precision.HIGHEST, preferred_element_type=jnp.float32)


def transition_blocks(site_rates):
    decay = jnp.exp(-site_rates)
    top = jnp.stack([decay * (1.0 + site_rates), decay], -1)
    bottom = jnp.stack([-decay * site_rates * site_rates, decay * (1.0 - site_rates)], -1)
    return jnp.stack([top, bottom], 1)


def apply_transition(values, site_rates):
    blocks = transition_blocks(site_rates)
    paired = values.reshape(site_rates.shape[0], 2, values.shape[-1])
    moved = jnp.einsum("scd,sdb->scb", blocks, paired, precision=lax.Precision.HIGHEST)
    return moved.reshape(values.shape)


def combine_levels(mapping, offset, toward):
    time_count = lax.axis_size("tm")
    time_index = lax.axis_index("tm")
    for level in range(time_count.bit_length() - 1):
        stride = 1 << level
        if toward > 0:
            active = time_index >= stride
        else:
            active = time_index + stride < time_count
        far_map, far_offset = shifted((mapping, offset), "tm", stride * toward)
        current = mapping
        joined_map = product(current, lax.all_gather(far_map, "rows", axis=0, tiled=True))
        joined_offset = (jnp.zeros_like(mapping), offset)[1] + product(
            current, lax.all_gather(far_offset, "rows", axis=0, tiled=True)
        )
        mapping = jnp.where(active, joined_map, mapping)
        offset = jnp.where(active, joined_offset, offset)
    return offset


def body(site_rates, prior_mean, observed, obs_mask, filter_gains, smooth_gains):
    time_count = lax.axis_size("tm")
    time_index = lax.axis_index("tm")
    row_index = lax.axis_index("rows")
    panel_rows = filter_gains.shape[1]
    site_count = site_rates.shape[0]
    state_dim = 2 * site_count
    panel_sites = panel_rows // 2
    start_site = row_index * panel_sites
    blocks = transition_blocks(site_rates)
    panel_blocks = lax.dynamic_slice_in_dim(blocks, start_site, panel_sites, 0)
    own_site = (
        jnp.arange(site_count)[None, :] == (start_site + jnp.arange(panel_sites))[:, None]
    ).astype(jnp.float32)
    trans_rows = (panel_blocks[:, :, None, :] * own_site[:, None, :, None]).reshape(
        panel_rows, state_dim
    )
    kept_gain = filter_gains[0] * obs_mask[0].astype(jnp.float32)[None, :]
    correction = jnp.stack(
        [kept_gain * blocks[:, 0, 0][None, :], kept_gain * blocks[:, 0, 1][None, :]], -1
    ).reshape(panel_rows, state_dim)
    step_map = trans_rows - correction
    drive = product(kept_gain, observed[0])
    at_start = time_index == 0
    mapping = jnp.where(at_start, jnp.zeros_like(step_map), step_map)
    offset = drive + jnp.where(at_start, product(step_map, prior_mean), jnp.zeros_like(drive))
    filtered = combine_levels(mapping, offset, 1)
    filt_full = lax.all_gather(filtered, "rows", axis=0, tiled=True)
    at_end = time_index == time_count - 1
    backward = jnp.where(at_end, jnp.zeros_like(smooth_gains[0]), smooth_gains[0])
    residual_term = filtered - product(backward, apply_transition(filt_full, site_rates))
    smoothed = combine_levels(backward, residual_term, -1)
    return (filtered[None], smoothed[None])


def solution(mesh):
    placed = (
        P(),
        P(),
        P("tm", None, None),
        P("tm", None),
        P("tm", "rows", None),
        P("tm", "rows", None),
    )
    return jax.shard_map(
        body,
        mesh=mesh,
        in_specs=placed,
        out_specs=(P("tm", "rows", None), P("tm", "rows", None)),
        check_vma=False,
    )
```

profile of v0, /device:TPU:75, one launch (start us, length us, event | category | flops | bytes accessed | tf_op | source)
XLA Modules:
  0.0 564.8 jit_solution(4351252597341530657)
XLA Ops:
  8.3 11.5 %broadcast_multiply_fusion = f32[128,2,256,2]{3,2,1,0:T(8,128)} fusion(f32[128,256]{1,0:T(8,128)S(1)} %fusion.22, f32[128,2,2]{2,1,0:T(2,128)S(1)} %copy.15), kind=kLoop, calls=%fused_computation | loop fusion | flops 131072 | bytes 657408 | tf_op jit(solution)/shard_map/mul | solution.py:65
  19.8 24.2 %mul.110 = f32[256,512]{1,0:T(8,128)S(1)} reshape(f32[128,2,256,2]{3,2,1,0:T(8,128)} %broadcast_multiply_fusion) | data formatting | bytes 1048576 | tf_op jit(solution)/shard_map/mul | solution.py:65
  48.1 11.6 %collective-permute-done.1 = f32[256,512]{1,0:T(8,128)S(1)} collective-permute-done((f32[256,512]{1,0:T(8,128)S(1)}, f32[256,512]{1,0:T(8,128)S(1)}, u32[]{:S(2)}, u32[]{:S(2)}) %collective-permute-start.1) | collective-permute-done | bytes 524320 | tf_op jit(solution)/shard_map/ppermute | solution.py:10
  60.6 18.2 %all-gather.13.cloned.1.call-done = f32[512,512]{1,0:T(8,128)} async-done(((f32[256,512]{1,0:T(8,128)}), f32[512,512]{1,0:T(8,128)}) %all-gather.13.cloned.1.call-update) | async-done | bytes 1048592 | tf_op jit(solution)/shard_map/all_gather | solution.py:42
  84.8 13.8 %collective-permute-done.3 = f32[256,512]{1,0:T(8,128)S(1)} collective-permute-done((f32[256,512]{1,0:T(8,128)S(1)}, f32[256,512]{1,0:T(8,128)S(1)}, u32[]{:S(2)}, u32[]{:S(2)}) %collective-permute-start.3) | collective-permute-done | bytes 524320 | tf_op jit(solution)/shard_map/ppermute | solution.py:10
  99.6 16.0 %all-gather.15.cloned.1.call-done = f32[512,512]{1,0:T(8,128)} async-done(((f32[256,512]{1,0:T(8,128)}), f32[512,512]{1,0:T(8,128)}) %all-gather.15.cloned.1.call-update) | async-done | bytes 1048592 | tf_op jit(solution)/shard_map/all_gather | solution.py:42
  121.0 12.1 %collective-permute-done.5 = f32[256,512]{1,0:T(8,128)} collective-permute-done((f32[256,512]{1,0:T(8,128)S(1)}, f32[256,512]{1,0:T(8,128)}, u32[]{:S(2)}, u32[]{:S(2)}) %collective-permute-start.5) | collective-permute-done | bytes 524320 | tf_op jit(solution)/shard_map/ppermute | solution.py:10
  138.3 10.4 %collective-permute-done.14 = f32[256,512]{1,0:T(8,128)} collective-permute-done((f32[256,512]{1,0:T(8,128)S(1)}, f32[256,512]{1,0:T(8,128)}, u32[]{:S(2)}, u32[]{:S(2)}) %collective-permute-start.14) | collective-permute-done | bytes 524320 | tf_op jit(solution)/shard_map/ppermute | solution.py:10
  175.1 9.3 %collective-permute-start.2 = (f32[256,384]{1,0:T(8,128)}, f32[256,384]{1,0:T(8,128)}, u32[]{:S(2)}, u32[]{:S(2)}) collective-permute-start(f32[256,384]{1,0:T(8,128)} %fusion.14), channel_id=1, source_target_pairs={{0,4},{2,6},{4,8},{6,10},{8,12},{10,14},{12,16},{14,18},{16,20},{1... | collective-permute-start | bytes 1179656 | tf_op jit(solution)/shard_map/ppermute | solution.py:10
  190.7 10.2 %all_gather.83 = f32[512,384]{1,0:T(8,128)} all-gather(f32[256,384]{1,0:T(8,128)} %collective-permute-done.2), channel_id=1, replica_groups=mesh['tm'=128,'rows'=2] {'rows'}, dimensions={0}, use_global_device_ids=true | all-gather | bytes 1179648 | tf_op jit(solution)/shard_map/all_gather | solution.py:44
  229.7 10.7 %collective-permute-start.6 = (f32[256,384]{1,0:T(8,128)}, f32[256,384]{1,0:T(8,128)}, u32[]{:S(2)}, u32[]{:S(2)}) collective-permute-start(f32[256,384]{1,0:T(8,128)} %fusion.12), channel_id=1, source_target_pairs={{0,16},{2,18},{4,20},{6,22},{8,24},{10,26},{12,28},{14,30},{16,32}... | collective-permute-start | bytes 1179656 | tf_op jit(solution)/shard_map/ppermute | solution.py:10
  279.1 13.5 %all_gather.89 = f32[512,384]{1,0:T(8,128)S(1)} all-gather(f32[256,384]{1,0:T(8,128)} %collective-permute-done.8), channel_id=1, replica_groups=mesh['tm'=128,'rows'=2] {'rows'}, dimensions={0}, use_global_device_ids=true | all-gather | bytes 1179648 | tf_op jit(solution)/shard_map/all_gather | solution.py:44
  295.4 8.0 %collective-permute-start.10 = (f32[256,384]{1,0:T(8,128)}, f32[256,384]{1,0:T(8,128)}, u32[]{:S(2)}, u32[]{:S(2)}) collective-permute-start(f32[256,384]{1,0:T(8,128)} %fusion.10), channel_id=1, source_target_pairs={{0,64},{2,66},{4,68},{6,70},{8,72},{10,74},{12,76},{14,78},{16,80}... | collective-permute-start | bytes 1179656 | tf_op jit(solution)/shard_map/ppermute | solution.py:10
  305.8 8.0 %collective-permute-start.20 = (f32[256,512]{1,0:T(8,128)S(1)}, f32[256,512]{1,0:T(8,128)}, u32[]{:S(2)}, u32[]{:S(2)}) collective-permute-start(f32[256,512]{1,0:T(8,128)S(1)} %convolution_select_fusion.3), channel_id=1, source_target_pairs={{16,0},{18,2},{20,4},{22,6},{24,8},{26,10},{28,12},{30,14},{32,16}... | collective-permute-start | bytes 1572872 | tf_op jit(solution)/shard_map/ppermute | solution.py:10
  326.4 8.0 %collective-permute-start.12 = (f32[256,384]{1,0:T(8,128)}, f32[256,384]{1,0:T(8,128)}, u32[]{:S(2)}, u32[]{:S(2)}) collective-permute-start(f32[256,384]{1,0:T(8,128)} %fusion.9), channel_id=1, source_target_pairs={{0,128},{2,130},{4,132},{6,134},{8,136},{10,138},{12,140},{14,142}... | collective-permute-start | bytes 1179656 | tf_op jit(solution)/shard_map/ppermute | solution.py:10
  335.4 15.1 %collective-permute-done.12 = f32[256,384]{1,0:T(8,128)} collective-permute-done((f32[256,384]{1,0:T(8,128)}, f32[256,384]{1,0:T(8,128)}, u32[]{:S(2)}, u32[]{:S(2)}) %collective-permute-start.12) | collective-permute-done | bytes 393248 | tf_op jit(solution)/shard_map/ppermute | solution.py:10
  395.1 9.8 %collective-permute-start.15 = (f32[256,384]{1,0:T(8,128)}, f32[256,384]{1,0:T(8,128)S(1)}, u32[]{:S(2)}, u32[]{:S(2)}) collective-permute-start(f32[256,384]{1,0:T(8,128)} %fusion.7), channel_id=1, source_target_pairs={{4,0},{6,2},{8,4},{10,6},{12,8},{14,10},{16,12},{18,14},{20,16},{2... | collective-permute-start | bytes 1179656 | tf_op jit(solution)/shard_map/ppermute | solution.py:10
  405.0 8.3 %collective-permute-done.15 = f32[256,384]{1,0:T(8,128)S(1)} collective-permute-done((f32[256,384]{1,0:T(8,128)}, f32[256,384]{1,0:T(8,128)S(1)}, u32[]{:S(2)}, u32[]{:S(2)}) %collective-permute-start.15) | collective-permute-done | bytes 393248 | tf_op jit(solution)/shard_map/ppermute | solution.py:10
  421.4 9.4 %collective-permute-done.17 = f32[256,384]{1,0:T(8,128)S(1)} collective-permute-done((f32[256,384]{1,0:T(8,128)S(1)}, f32[256,384]{1,0:T(8,128)S(1)}, u32[]{:S(2)}, u32[]{:S(2)}) %collective-permute-start.17) | collective-permute-done | bytes 393248 | tf_op jit(solution)/shard_map/ppermute | solution.py:10
  443.3 8.9 %collective-permute-done.19 = f32[256,384]{1,0:T(8,128)} collective-permute-done((f32[256,384]{1,0:T(8,128)S(1)}, f32[256,384]{1,0:T(8,128)}, u32[]{:S(2)}, u32[]{:S(2)}) %collective-permute-start.19) | collective-permute-done | bytes 393248 | tf_op jit(solution)/shard_map/ppermute | solution.py:10
  460.3 10.8 %collective-permute-done.24 = f32[256,512]{1,0:T(8,128)} collective-permute-done((f32[256,512]{1,0:T(8,128)S(1)}, f32[256,512]{1,0:T(8,128)}, u32[]{:S(2)}, u32[]{:S(2)}) %collective-permute-start.24) | collective-permute-done | bytes 524320 | tf_op jit(solution)/shard_map/ppermute | solution.py:10
  471.1 12.8 %collective-permute-done.21 = f32[256,384]{1,0:T(8,128)S(1)} collective-permute-done((f32[256,384]{1,0:T(8,128)}, f32[256,384]{1,0:T(8,128)S(1)}, u32[]{:S(2)}, u32[]{:S(2)}) %collective-permute-start.21) | collective-permute-done | bytes 393248 | tf_op jit(solution)/shard_map/ppermute | solution.py:10
  491.1 38.3 %collective-permute-done.23 = f32[256,384]{1,0:T(8,128)S(1)} collective-permute-done((f32[256,384]{1,0:T(8,128)S(1)}, f32[256,384]{1,0:T(8,128)S(1)}, u32[]{:S(2)}, u32[]{:S(2)}) %collective-permute-start.23) | collective-permute-done | bytes 393248 | tf_op jit(solution)/shard_map/ppermute | solution.py:10
  536.5 16.8 %collective-permute-done.25 = f32[256,384]{1,0:T(8,128)S(1)} collective-permute-done((f32[256,384]{1,0:T(8,128)S(1)}, f32[256,384]{1,0:T(8,128)S(1)}, u32[]{:S(2)}, u32[]{:S(2)}) %collective-permute-start.25) | collective-permute-done | bytes 393248 | tf_op jit(solution)/shard_map/ppermute | solution.py:10
  (146 shorter events, 233.7 us)
Async XLA Ops:
  7.2 71.7 %all-gather.13.cloned.1.call-start = ((), (), s32[]{:S(2)}) async-start(), calls=%async_computation | async-start | bytes 1572864 | tf_op jit(solution)/shard_map/all_gather | solution.py:42
  60.5 55.0 %all-gather.15.cloned.1.call-start = ((), (), s32[]{:S(2)}) async-start(), calls=%async_computation.1 | async-start | bytes 1572864 | tf_op jit(solution)/shard_map/all_gather | solution.py:42
  99.5 54.3 %all-gather.17.cloned.1.call-start = ((), (), s32[]{:S(2)}) async-start(), calls=%async_computation.2 | async-start | bytes 1572864 | tf_op jit(solution)/shard_map/all_gather | solution.py:42
  133.1 51.3 %all-gather.25.cloned.1.call-start = ((), (), s32[]{:S(2)}) async-start(), calls=%async_computation.6 | async-start | bytes 1572864 | tf_op jit(solution)/shard_map/all_gather | solution.py:42
  148.7 60.3 %all-gather.19.cloned.1.call-start = ((), (), s32[]{:S(2)}) async-start(), calls=%async_computation.3 | async-start | bytes 1572864 | tf_op jit(solution)/shard_map/all_gather | solution.py:42
  172.0 68.5 %all-gather.27.cloned.1.call-start = ((), (), s32[]{:S(2)}) async-start(), calls=%async_computation.7 | async-start | bytes 1572864 | tf_op jit(solution)/shard_map/all_gather | solution.py:42
  203.8 65.1 %all-gather.21.cloned.1.call-start = ((), (), s32[]{:S(2)}) async-start(), calls=%async_computation.4 | async-start | bytes 1572864 | tf_op jit(solution)/shard_map/all_gather | solution.py:42
  226.7 76.9 %all-gather.29.cloned.1.call-start = ((), (), s32[]{:S(2)}) async-start(), calls=%async_computation.8 | async-start | bytes 1572864 | tf_op jit(solution)/shard_map/all_gather | solution.py:42
  229.7 19.8 %collective-permute-start.6 = (f32[256,384]{1,0:T(8,128)}, f32[256,384]{1,0:T(8,128)}, u32[]{:S(2)}, u32[]{:S(2)}) collective-permute-start(f32[256,384]{1,0:T(8,128)} %fusion.12), channel_id=1, source_target_pairs={{0,16},{2,18},{4,20},{6,22},{8,24},{10,26},{12,28},{14,30},{16,32}... | collective-permute-start | bytes 1179656 | tf_op jit(solution)/shard_map/ppermute | solution.py:10
  242.7 18.8 %collective-permute-start.18 = (f32[256,512]{1,0:T(8,128)S(1)}, f32[256,512]{1,0:T(8,128)}, u32[]{:S(2)}, u32[]{:S(2)}) collective-permute-start(f32[256,512]{1,0:T(8,128)S(1)} %convolution_select_fusion.4), channel_id=1, source_target_pairs={{8,0},{10,2},{12,4},{14,6},{16,8},{18,10},{20,12},{22,14},{24,16},... | collective-permute-start | bytes 1572872 | tf_op jit(solution)/shard_map/ppermute | solution.py:10
  261.6 94.0 %all-gather.23.cloned.1.call-start = ((), (), s32[]{:S(2)}) async-start(), calls=%async_computation.5 | async-start | bytes 1572864 | tf_op jit(solution)/shard_map/all_gather | solution.py:42
  271.2 32.3 %collective-permute-start.11 = (f32[256,512]{1,0:T(8,128)S(1)}, f32[256,512]{1,0:T(8,128)}, u32[]{:S(2)}, u32[]{:S(2)}) collective-permute-start(f32[256,512]{1,0:T(8,128)S(1)} %convolution_select_fusion.7), channel_id=1, source_target_pairs={{0,64},{2,66},{4,68},{6,70},{8,72},{10,74},{12,76},{14,78},{16,80}... | collective-permute-start | bytes 1572872 | tf_op jit(solution)/shard_map/ppermute | solution.py:10
  295.4 24.8 %collective-permute-start.10 = (f32[256,384]{1,0:T(8,128)}, f32[256,384]{1,0:T(8,128)}, u32[]{:S(2)}, u32[]{:S(2)}) collective-permute-start(f32[256,384]{1,0:T(8,128)} %fusion.10), channel_id=1, source_target_pairs={{0,64},{2,66},{4,68},{6,70},{8,72},{10,74},{12,76},{14,78},{16,80}... | collective-permute-start | bytes 1179656 | tf_op jit(solution)/shard_map/ppermute | solution.py:10
  303.5 76.7 %all-gather.31.cloned.1.call-start = ((), (), s32[]{:S(2)}) async-start(), calls=%async_computation.9 | async-start | bytes 1572864 | tf_op jit(solution)/shard_map/all_gather | solution.py:42
  305.8 29.5 %collective-permute-start.20 = (f32[256,512]{1,0:T(8,128)S(1)}, f32[256,512]{1,0:T(8,128)}, u32[]{:S(2)}, u32[]{:S(2)}) collective-permute-start(f32[256,512]{1,0:T(8,128)S(1)} %convolution_select_fusion.3), channel_id=1, source_target_pairs={{16,0},{18,2},{20,4},{22,6},{24,8},{26,10},{28,12},{30,14},{32,16}... | collective-permute-start | bytes 1572872 | tf_op jit(solution)/shard_map/ppermute | solution.py:10
  326.4 24.1 %collective-permute-start.12 = (f32[256,384]{1,0:T(8,128)}, f32[256,384]{1,0:T(8,128)}, u32[]{:S(2)}, u32[]{:S(2)}) collective-permute-start(f32[256,384]{1,0:T(8,128)} %fusion.9), channel_id=1, source_target_pairs={{0,128},{2,130},{4,132},{6,134},{8,136},{10,138},{12,140},{14,142}... | collective-permute-start | bytes 1179656 | tf_op jit(solution)/shard_map/ppermute | solution.py:10
  335.3 103.7 %all-gather.33.cloned.1.call-start = ((), (), s32[]{:S(2)}) async-start(), calls=%async_computation.10 | async-start | bytes 1572864 | tf_op jit(solution)/shard_map/all_gather | solution.py:42
  382.5 22.4 %collective-permute-start.22 = (f32[256,512]{1,0:T(8,128)S(1)}, f32[256,512]{1,0:T(8,128)}, u32[]{:S(2)}, u32[]{:S(2)}) collective-permute-start(f32[256,512]{1,0:T(8,128)S(1)} %convolution_select_fusion.2), channel_id=1, source_target_pairs={{32,0},{34,2},{36,4},{38,6},{40,8},{42,10},{44,12},{46,14},{48,16}... | collective-permute-start | bytes 1572872 | tf_op jit(solution)/shard_map/ppermute | solution.py:10
  395.1 18.2 %collective-permute-start.15 = (f32[256,384]{1,0:T(8,128)}, f32[256,384]{1,0:T(8,128)S(1)}, u32[]{:S(2)}, u32[]{:S(2)}) collective-permute-start(f32[256,384]{1,0:T(8,128)} %fusion.7), channel_id=1, source_target_pairs={{4,0},{6,2},{8,4},{10,6},{12,8},{14,10},{16,12},{18,14},{20,16},{2... | collective-permute-start | bytes 1179656 | tf_op jit(solution)/shard_map/ppermute | solution.py:10
  404.9 129.3 %all-gather.35.cloned.1.call-start = ((), (), s32[]{:S(2)}) async-start(), calls=%async_computation.11 | async-start | bytes 1572864 | tf_op jit(solution)/shard_map/all_gather | solution.py:42
  441.4 29.8 %collective-permute-start.24 = (f32[256,512]{1,0:T(8,128)S(1)}, f32[256,512]{1,0:T(8,128)}, u32[]{:S(2)}, u32[]{:S(2)}) collective-permute-start(f32[256,512]{1,0:T(8,128)S(1)} %convolution_select_fusion.1), channel_id=1, source_target_pairs={{64,0},{66,2},{68,4},{70,6},{72,8},{74,10},{76,12},{78,14},{80,16}... | collective-permute-start | bytes 1572872 | tf_op jit(solution)/shard_map/ppermute | solution.py:10
  458.4 25.6 %collective-permute-start.21 = (f32[256,384]{1,0:T(8,128)}, f32[256,384]{1,0:T(8,128)S(1)}, u32[]{:S(2)}, u32[]{:S(2)}) collective-permute-start(f32[256,384]{1,0:T(8,128)} %fusion.4), channel_id=1, source_target_pairs={{32,0},{34,2},{36,4},{38,6},{40,8},{42,10},{44,12},{46,14},{48,16}... | collective-permute-start | bytes 1179656 | tf_op jit(solution)/shard_map/ppermute | solution.py:10
  489.2 40.2 %collective-permute-start.23 = (f32[256,384]{1,0:T(8,128)S(1)}, f32[256,384]{1,0:T(8,128)S(1)}, u32[]{:S(2)}, u32[]{:S(2)}) collective-permute-start(f32[256,384]{1,0:T(8,128)S(1)} %fusion.3), channel_id=1, source_target_pairs={{64,0},{66,2},{68,4},{70,6},{72,8},{74,10},{76,12},{78,14},{80,16}... | collective-permute-start | bytes 1179656 | tf_op jit(solution)/shard_map/ppermute | solution.py:10
  532.9 20.4 %collective-permute-start.25 = (f32[256,384]{1,0:T(8,128)S(1)}, f32[256,384]{1,0:T(8,128)S(1)}, u32[]{:S(2)}, u32[]{:S(2)}) collective-permute-start(f32[256,384]{1,0:T(8,128)S(1)} %fusion.2), channel_id=1, source_target_pairs={{128,0},{130,2},{132,4},{134,6},{136,8},{138,10},{140,12},{142,14}... | collective-permute-start | bytes 1179656 | tf_op jit(solution)/shard_map/ppermute | solution.py:10
  (22 other events, 527.0 us)
Sparse Core Ops, SparseCore 0:
  60.7 18.1 all-gather.12
  99.6 15.8 all-gather.14
  133.2 17.4 all-gather.16
  152.4 17.4 all-gather.24
  172.1 22.9 all-gather.18
  204.0 22.5 all-gather.26
  228.3 26.9 all-gather.20
  261.7 21.9 all-gather.28
  303.6 23.2 all-gather.22
  335.5 16.9 all-gather.30
  405.1 16.6 all-gather.32
  471.3 21.1 all-gather.34
where the time goes:
time: 576 us; the launch traced here: 565 us
  waiting for transfers between devices  240 us (42%)
  starting transfers between devices  114 us (20%)
  blocking collectives  75.7 us (13%)
  matrix products  72.8 us (13%)
  local copies, waits for them, and re-layouts  32.7 us (6%)
  between operations  15.4 us (3%)
  other arithmetic  13.6 us (2%)
    ppermute x26, waiting for transfers between devices, shifted(): lax.ppermute(value, axis, [(source, source + steps) for source in range(f...  206 us
    ppermute x26, starting transfers between devices, shifted(): lax.ppermute(value, axis, [(source, source + steps) for source in range(f...  114 us
    all_gather x14, blocking collectives, combine_levels(): lax.all_gather(far_offset, 'rows', axis=0, tiled=True)  73 us
    dot_general x29, matrix products, product(): jnp.dot(left, right, precision=lax.Precision.HIGHEST, preferred_element_t...  67.2 us
    all_gather x12, waiting for transfers between devices, combine_levels(): lax.all_gather(far_map, 'rows', axis=0, tiled=True)  34.4 us
    mul x1, local copies, waits for them, and re-layouts, body(): panel_blocks[:, :, None, :] * own_site[:, None, :, None]  24.2 us
  transfers between devices with their start and end apart: 38, of which 23 were waited for; matrix products, arithmetic and copies ran while one was open for 13% of the time, Pallas kernels for 0%

commit v1 on v0

v1 whole, which is shorter than its diff:
```python
import functools

import jax
import jax.numpy as jnp
from jax import lax
from jax.experimental import pallas as pl
from jax.experimental.pallas import tpu as pltpu
from jax.sharding import PartitionSpec as P

F32, BF16 = jnp.float32, jnp.bfloat16
SIDE = 4
STEPS = SIDE * SIDE
LANE = 128
PAD = 16


def halves(value):
    high = value.astype(BF16)
    return high, (value - high.astype(F32)).astype(BF16)


def product(left, right):
    dot = functools.partial(jnp.dot, preferred_element_type=F32)
    left_high, left_low = halves(left)
    right_high, right_low = halves(right)
    rows = left.shape[0]
    both = dot(jnp.concatenate([left_high, left_low], 0), right_high)
    return both[:rows] + (both[rows:] + dot(left_high, right_low))


class Place:
    def __init__(self, blocks):
        time = lax.axis_index("tm")
        self.blocks = blocks
        self.z, self.q = lax.div(time, STEPS), lax.rem(time, STEPS)
        self.y, self.x = lax.div(self.q, SIDE), lax.rem(self.q, SIDE)
        self.core = lax.axis_index("rows")
        self.partner = {"tm": time, "rows": 1 - self.core}

    def chip(self, dy, dx):
        return lax.rem(self.y + dy % SIDE, SIDE) * SIDE + lax.rem(self.x + dx % SIDE, SIDE)

    def device(self, q, core):
        return {"tm": self.z * STEPS + q, "rows": core}

    def above(self, dz):
        z = lax.rem(self.z + dz % self.blocks, self.blocks)
        return {"tm": z * STEPS + self.q, "rows": self.core}


def remote(src, dst, send, recv, device):
    return pltpu.make_async_remote_copy(
        src_ref=src, dst_ref=dst, send_sem=send, recv_sem=recv, device_id=device, device_id_type=pl.DeviceIdType.MESH
    )


def gather_plane(place, own, buf, send, recv, side_send, side_recv, local):
    core, rows = place.core, own.shape[0]
    half, quarter = rows // 2, rows // 4
    axes = ((0, 1), (1, 0))
    started, index = {}, [0]

    def off(*terms):
        return tuple(sum(scale * axis[i] for scale, axis in terms) for i in (0, 1))

    def view(offset, start, size):
        return buf.at[place.chip(*offset), core, pl.ds(start, size)]

    def begin(key, offset, start, size, to, mine=False):
        src = own.at[pl.ds(start, size)] if mine else view(offset, start, size)
        i = index[0]
        index[0] += 1
        copy = remote(src, view(offset, start, size), send.at[i], recv.at[i], place.device(place.chip(*to), core))
        copy.start()
        started[key] = copy

    def across(offset, h):
        i = h * STEPS + (offset[0] % SIDE) * SIDE + offset[1] % SIDE
        mine = offset == (0, 0)
        src = own.at[pl.ds(h * half, half)] if mine else view(offset, h * half, half)
        copy = remote(src, view(offset, h * half, half), side_send.at[i], side_recv.at[i], place.partner)
        copy.start()
        started["side", i] = copy

    keep = pltpu.make_async_copy(own, buf.at[place.q, core], local)
    keep.start()
    for h in (0, 1):
        for s in (1, -1):
            begin(("a1", h, s), (0, 0), h * half, half, off((s, axes[h])), True)
    for h in (0, 1):
        for s in (1, -1):
            begin(("b1", h, 0, s), (0, 0), h * half, half, off((s, axes[1 - h])), True)
    for h in (0, 1):
        across((0, 0), h)
    yield
    for s in (1, -1):
        for h in (0, 1):
            a, b = axes[h], axes[1 - h]
            started["a1", h, s].wait_recv()
            came = off((-s, a))
            begin(("a2", h, s), came, h * half + (quarter if s < 0 else 0), quarter, off((s, a)))
            for t in (1, -1):
                begin(("b1", h, -s, t), came, h * half, half, off((t, b)))
            across(came, h)
            yield

    def second(h, o, s):
        a, b = axes[h], axes[1 - h]
        started["b1", h, o, s].wait_recv()
        came = off((o, a), (-s, b))
        begin(("b2", h, o, s), came, h * half + (quarter if s < 0 else 0), quarter, off((s, b)))
        across(came, h)

    for s in (1, -1):
        for h in (0, 1):
            second(h, 0, s)
            yield
    for h in (0, 1):
        for s in (1, -1):
            started["a2", h, s].wait_recv()
        came = off((2, axes[h]))
        for t in (1, -1):
            begin(("b1", h, 2, t), came, h * half, half, off((t, axes[1 - h])))
        across(came, h)
        yield
    for o in (-1, 1, 2):
        for s in (1, -1):
            for h in (0, 1):
                second(h, o, s)
                yield
    for o in (0, -1, 1, 2):
        for h in (0, 1):
            for s in (1, -1):
                started["b2", h, o, s].wait_recv()
            across(off((o, axes[h]), (2, axes[1 - h])), h)
            yield
    for i in range(2 * STEPS):
        started["side", i].wait_recv()
    keep.wait()
    for copy in started.values():
        copy.wait_send()
    yield


def gather_rows(place, stage, buf, send, recv, side_send, side_recv, local):
    core = place.core
    keep = pltpu.make_async_copy(stage, buf.at[place.q, core], local)
    keep.start()
    copies, sides = [], []
    order = sorted(range(1, STEPS), key=lambda i: -sum(min(k, SIDE - k) for k in divmod(i, SIDE)))
    for i in order:
        copy = remote(stage, buf.at[place.q, core], send.at[i], recv.at[i],
                      place.device(place.chip(*divmod(i, SIDE)), core))
        copy.start()
        copies.append(copy)

    def across(i, src):
        dy, dx = divmod(i, SIDE)
        dst = buf.at[place.chip(-dy, -dx), core]
        copy = remote(dst if src is None else src, dst, side_send.at[i], side_recv.at[i], place.partner)
        copy.start()
        sides.append(copy)

    across(0, stage)
    for i, copy in reversed(list(zip(order, copies))):
        copy.wait_recv()
        across(i, None)
    for copy in sides:
        copy.wait_recv()
    keep.wait()
    for copy in copies + sides:
        copy.wait_send()


def kernel(blocks, gain, back, obs, prior, coef, filt, smooth,
           gains, backs, seen, kept, pmap, qmap, stage, enter, leave, turn, far, sout, fsend,
           ksend, krecv, kside_s, kside_r, gsend, grecv, gside_s, gside_r,
           osend, orecv, msend, mrecv, mside_s, mside_r, chain, fsem, ssem, local):
    place = Place(blocks)
    core = place.core
    barrier = pltpu.get_barrier_semaphore()
    greet = [place.partner, place.above(1), place.above(-1)]
    for i in range(1, STEPS):
        q = place.chip(*divmod(i, SIDE))
        greet += [place.device(q, core), place.device(q, 1 - core)]
    for device in greet:
        pl.semaphore_signal(barrier, inc=1, device_id=device, device_id_type=pl.DeviceIdType.MESH)
    pl.semaphore_wait(barrier, len(greet))

    watch = []
    for i in range(1, STEPS):
        q = place.chip(*divmod(i, SIDE))
        copy = remote(obs.at[q, core], seen.at[place.q], osend.at[i], orecv.at[i], place.device(q, core))
        copy.start()
        watch.append(copy)
    own_obs = pltpu.make_async_copy(obs.at[place.q, core], seen.at[place.q], local.at[0])
    own_obs.start()

    first = gather_plane(place, gain, gains, ksend, krecv, kside_s, kside_r, local.at[1])
    for _ in first:
        pass
    for copy in watch:
        copy.wait()
    own_obs.wait()
    second = gather_plane(place, back, backs, gsend, grecv, gside_s, gside_r, local.at[2])
    next(second)

    alpha, beta = coef[0:1, :], coef[1:2, :]

    def moved(state):
        swap = jnp.concatenate([state[:, i * LANE:(i + 1) * LANE] for i in (1, 0, 3, 2)], 1)
        return alpha * state + beta * swap

    def values(state):
        return jnp.concatenate([state[:, :LANE], state[:, 2 * LANE:3 * LANE]], 1)

    row = lax.broadcasted_iota(jnp.int32, (PAD, 4 * LANE), 0)
    lane = lax.broadcasted_iota(jnp.int32, (PAD, 4 * LANE), 1)
    unit = jnp.where(lane == row + (place.q * 2 + core) * PAD, 1.0, 0.0).astype(F32)
    zero = jnp.zeros((PAD, 4 * LANE), F32)

    def forward(k, state, rows):
        predicted = moved(state)
        target = seen[k]
        if rows > PAD:
            target = jnp.concatenate([target, jnp.zeros((rows - PAD, 2 * LANE), F32)], 0)
        innovation = target - values(predicted)
        return predicted + jnp.concatenate([product(innovation, gains[k, half]) for half in (0, 1)], 1)

    both = lax.fori_loop(0, STEPS, lambda k, state: forward(k, state, 2 * PAD), jnp.concatenate([zero, unit], 0))
    stage[...] = both[PAD:]
    leave[...] = both[:PAD]
    for _ in second:
        pass
    gather_rows(place, stage, pmap, msend.at[0], mrecv.at[0], mside_s.at[0], mside_r.at[0], local.at[3])

    def mapped(state, table):
        return product(state, table[...].reshape(4 * LANE, 4 * LANE))

    up = remote(leave, enter, chain.at[0], chain.at[1], place.above(1))

    @pl.when(place.z == 0)
    def _():
        enter[...] = prior[...]

    @pl.when(place.z > 0)
    def _():
        up.wait_recv()

    @pl.when(place.z < blocks - 1)
    def _():
        leave[...] = leave[...] + mapped(enter[...], pmap)
        up.start()

    def hand_on(value_ref, k, out, sem):
        for half in (0, 1):
            part = value_ref.at[k, half]
            home = jnp.logical_and(k == place.q, core == half)

            @pl.when(home)
            def _():
                pltpu.make_async_copy(part, out.at[place.q, core], sem.at[1]).start()

            @pl.when(jnp.logical_not(home))
            def _():
                remote(part, out.at[place.q, core], sem.at[0], sem.at[1], place.device(k, half)).start()

    def all_handed(out, sem):
        pltpu.make_async_copy(out, out, sem.at[1]).wait()
        rest = out.at[pl.ds(0, STEPS - 1)]
        pltpu.make_async_copy(rest, rest, sem.at[0]).wait()
        pltpu.make_async_copy(out.at[0, 0], out.at[0, 0], sem.at[0]).wait()

    def filter_step(k, state):
        state = forward(k, state, PAD)
        kept[k] = state
        fsend[k, 0] = state[:, :2 * LANE]
        fsend[k, 1] = state[:, 2 * LANE:]
        hand_on(fsend, k, filt, fsem)
        return state

    lax.fori_loop(0, STEPS, filter_step, enter[...])

    @pl.when(place.z < blocks - 1)
    def _():
        up.wait_send()

    def smoothed(k, ahead):
        wanted = ahead - moved(kept[k])
        return kept[k] + back_product(k, wanted)

    def back_product(k, value):
        return jnp.concatenate([product(value, backs[k, half]) for half in (0, 1)], 1)

    def both_back(i, state):
        k = STEPS - 1 - i
        held = kept[k]
        wanted = jnp.concatenate([state[:PAD] - moved(held), state[PAD:]], 0)
        return jnp.concatenate([held, zero], 0) + back_product(k, wanted)

    both = lax.fori_loop(0, STEPS, both_back, jnp.concatenate([zero, unit], 0))
    turn[...] = both[PAD:]
    far[0] = both[:PAD]
    gather_rows(place, turn, qmap, msend.at[1], mrecv.at[1], mside_s.at[1], mside_r.at[1], local.at[4])

    down = remote(far.at[0], far.at[1], chain.at[2], chain.at[3], place.above(-1))

    @pl.when(place.z == blocks - 1)
    def _():
        far[1] = zero

    @pl.when(place.z < blocks - 1)
    def _():
        down.wait_recv()

    @pl.when(place.z > 0)
    def _():
        far[0] = far[0] + mapped(far[1], qmap)
        down.start()

    def smooth_step(i, state):
        k = STEPS - 1 - i
        state = smoothed(k, state)
        sout[k, 0] = state[:, :2 * LANE]
        sout[k, 1] = state[:, 2 * LANE:]
        hand_on(sout, k, smooth, ssem)
        return state

    lax.fori_loop(0, STEPS, smooth_step, far[1])

    @pl.when(place.z > 0)
    def _():
        down.wait_send()

    all_handed(filt, fsem)
    all_handed(smooth, ssem)


def transition_blocks(site_rates):
    decay = jnp.exp(-site_rates)
    top = jnp.stack([decay * (1.0 + site_rates), decay], -1)
    bottom = jnp.stack([-decay * site_rates * site_rates, decay * (1.0 - site_rates)], -1)
    return jnp.stack([top, bottom], 1)


def state_order(rows):
    return rows.reshape(2, LANE, 2, -1).transpose(0, 2, 1, 3).reshape(4 * LANE, -1)


def body(site_rates, prior_mean, observed, obs_mask, filter_gains, smooth_gains):
    time_count, time_index = lax.axis_size("tm"), lax.axis_index("tm")
    blocks = time_count // STEPS
    core = lax.axis_index("rows")
    paths = prior_mean.shape[1]
    share = paths // (2 * STEPS)
    table = transition_blocks(site_rates)
    alpha = state_order(jnp.stack([table[:, 0, 0], table[:, 1, 1]], 1).reshape(-1, 1)).T
    beta = state_order(jnp.stack([table[:, 0, 1], table[:, 1, 0]], 1).reshape(-1, 1)).T
    coef = jnp.concatenate([alpha, beta, jnp.zeros((6, 4 * LANE), F32)], 0)
    gain = filter_gains[0] * obs_mask[0].astype(F32)[None, :]
    gain = gain.reshape(LANE, 2, 2 * LANE).transpose(2, 1, 0).reshape(2 * LANE, 2 * LANE)
    back = jnp.where(time_index == time_count - 1, 0.0, smooth_gains[0])
    back = back.reshape(LANE, 2, 2, LANE, 2).transpose(2, 4, 3, 1, 0).reshape(4 * LANE, 2 * LANE)
    pad = ((0, 0), (0, PAD - share), (0, 0))
    obs = jnp.pad(observed[0].T.reshape(2 * STEPS, share, 2 * LANE), pad).reshape(STEPS, 2, PAD, 2 * LANE)
    mine = (lax.rem(time_index, STEPS) * 2 + core) * share
    prior = state_order(lax.dynamic_slice_in_dim(prior_mean, mine, share, 1)).T
    prior = jnp.pad(prior, ((0, PAD - share), (0, 0)))

    vmem = pl.BlockSpec(memory_space=pltpu.VMEM)
    dma, out = pltpu.SemaphoreType.DMA, jax.ShapeDtypeStruct((STEPS, 2, PAD, 2 * LANE), F32)
    filt, smooth = pl.pallas_call(
        functools.partial(kernel, blocks),
        out_shape=(out, out),
        in_specs=[vmem] * 5,
        out_specs=(vmem, vmem),
        scratch_shapes=[
            pltpu.VMEM((STEPS, 2, 2 * LANE, 2 * LANE), F32),
            pltpu.VMEM((STEPS, 2, 4 * LANE, 2 * LANE), F32),
            pltpu.VMEM((STEPS, PAD, 2 * LANE), F32),
            pltpu.VMEM((STEPS, PAD, 4 * LANE), F32),
            pltpu.VMEM((STEPS, 2, PAD, 4 * LANE), F32),
            pltpu.VMEM((STEPS, 2, PAD, 4 * LANE), F32),
            pltpu.VMEM((PAD, 4 * LANE), F32),
            pltpu.VMEM((PAD, 4 * LANE), F32),
            pltpu.VMEM((PAD, 4 * LANE), F32),
            pltpu.VMEM((PAD, 4 * LANE), F32),
            pltpu.VMEM((2, PAD, 4 * LANE), F32),
            pltpu.VMEM((STEPS, 2, PAD, 2 * LANE), F32),
            pltpu.VMEM((STEPS, 2, PAD, 2 * LANE), F32),
            dma((40,)), dma((40,)), dma((32,)), dma((32,)),
            dma((40,)), dma((40,)), dma((32,)), dma((32,)),
            dma((STEPS,)), dma((STEPS,)),
            dma((2, STEPS)), dma((2, STEPS)), dma((2, STEPS)), dma((2, STEPS)),
            dma((4,)), dma((2,)), dma((2,)), dma((5,)),
        ],
        compiler_params=pltpu.CompilerParams(
            collective_id=0, has_side_effects=True, vmem_limit_bytes=60 * 1024 * 1024
        ),
        name="two_level_scan",
    )(gain, back, obs, prior, coef)

    def placed(value):
        rows = value.reshape(2 * STEPS, PAD, 2 * LANE)[:, :share].reshape(paths, 2, LANE)
        return rows.transpose(2, 1, 0).reshape(1, 2 * LANE, paths)

    return placed(filt), placed(smooth)


def solution(mesh):
    placed = (
        P(),
        P(),
        P("tm", None, None),
        P("tm", None),
        P("tm", "rows", None),
        P("tm", "rows", None),
    )
    return jax.shard_map(
        body,
        mesh=mesh,
        in_specs=placed,
        out_specs=(P("tm", "rows", None), P("tm", "rows", None)),
        check_vma=False,
    )
```

time: 576 us -> 244 us (0.42)
  the two profiles are of different devices: /device:TPU:75 before, /device:TPU:1 now
where the time goes in v1:
time: 244 us
  Pallas kernels  172 us (70%)
  local copies, waits for them, and re-layouts  68.2 us (28%)
  other arithmetic  2.49 us (1%)
    pallas_call x1, Pallas kernels, body(): pl.pallas_call(functools.partial(kernel, blocks), out_shape=(out, out), i...  172 us
    select_n x1, local copies, waits for them, and re-layouts, body(): back = jnp.where(time_index == time_count - 1, 0.0, smooth_gains[0])  34.8 us
    transpose x1, local copies, waits for them, and re-layouts, body(): back.reshape(LANE, 2, 2, LANE, 2).transpose(2, 4, 3, 1, 0)  23.4 us

profile of v1, /device:TPU:1, one launch (start us, length us, event | category | flops | bytes accessed | tf_op | source)
XLA Modules:
  0.0 243.6 jit_solution(14311395992897133429)
XLA Ops:
  0.6 0.0 copy-start
  0.7 1.1 copy-done
  1.8 0.1 constant_dynamic-slice_fusion
  1.9 0.1 copy.33
  2.1 0.6 pad.9.prior
  2.7 0.7 add_multiply_fusion
  3.5 0.1 pad.12.clone
  3.5 0.7 maximum_maximum_fusion.coef
  4.2 1.1 broadcast_select_fusion
  5.3 0.0 copy-start.1
  5.3 34.8 %select_n.17 = f32[128,2,2,128,2]{4,3,2,1,0:T(8,128)} reshape(f32[1,256,512]{2,1,0:T(8,128)S(1)} %broadcast_select_fusion) | data formatting | bytes 1048576 | tf_op jit(solution)/shard_map/jit(_where)/select_n | solution.py:362
  40.1 23.4 %copy.31 = f32[2,2,128,2,128]{4,3,2,1,0:T(2,128)S(1)} copy(f32[2,2,128,2,128]{1,2,0,3,4:T(8,128)} %bitcast.48) | data formatting | bytes 1048576 | tf_op jit(solution)/shard_map/transpose | solution.py:363
  63.6 0.8 copy.40
  64.4 0.2 copy.32
  64.6 0.8 pad.8
  65.5 0.1 squeeze.8
  65.7 0.8 copy.36.gain
  66.5 172.2 %two_level_scan.1 = (f32[16,2,16,256]{3,2,1,0:T(8,128)}, f32[16,2,16,256]{3,2,1,0:T(8,128)}) custom-call(f32[256,256]{1,0:T(8,128)} %copy.36.gain, f32[512,256]{1,0:T(8,128)} %bitcast.50, f32[16,2,16,256]{3,2,1,0:T(8,128)} %bitcast.51, f32[16,512]{1,0:T(8,128)} %pad.9.prior, f32[8,512]{1,0:T(8,128)} %maximum_maximum_fusion.coef), custom_call_target="tpu_custom_call" | custom-call | tf_op jit(solution)/shard_map/two_level_scan/pallas_call | solution.py:372
  238.7 1.2 reshape.67
  239.9 0.2 copy.34
  240.2 1.0 reshape.68
  241.2 1.2 reshape.70
  242.4 0.2 copy.35
  242.6 1.0 reshape.71
  (15 shorter events, 0.2 us)
Async XLA Ops:
  0.6 1.1 copy-start
  5.3 59.1 %copy-start.1 = (f32[1,256,384]{2,1,0:T(8,128)S(1)}, f32[1,256,384]{2,1,0:T(8,128)}, u32[]{:S(2)}) copy-start(f32[1,256,384]{2,1,0:T(8,128)} %param.8) | copy-start | bytes 1179652
  5.3 60.2 %copy-start.2 = (f32[1,256,256]{2,1,0:T(8,128)S(1)}, f32[1,256,256]{2,1,0:T(8,128)}, u32[]{:S(2)}) copy-start(f32[1,256,256]{2,1,0:T(8,128)} %param.10) | copy-start | bytes 786436
  5.3 60.3 %copy-start.3 = (s32[1,256]{1,0:T(1,128)S(1)}, s32[1,256]{1,0:T(1,128)}, u32[]{:S(2)}) copy-start(s32[1,256]{1,0:T(1,128)} %param.9) | copy-start | bytes 3076

commit v2 on v0

v2 whole, which is shorter than its diff:
```python
import functools

import jax
import jax.numpy as jnp
from jax import lax
from jax.experimental import pallas as pl
from jax.experimental.pallas import tpu as pltpu
from jax.sharding import PartitionSpec as P

F32, BF16 = jnp.float32, jnp.bfloat16
SIDE = 4
STEPS = SIDE * SIDE
LANE = 128
PAD = 16


def halves(value):
    high = value.astype(BF16)
    return high, (value - high.astype(F32)).astype(BF16)


def product(left, right):
    dot = functools.partial(jnp.dot, preferred_element_type=F32)
    left_high, left_low = halves(left)
    right_high, right_low = halves(right)
    rows = left.shape[0]
    both = dot(jnp.concatenate([left_high, left_low], 0), right_high)
    return both[:rows] + (both[rows:] + dot(left_high, right_low))


class Place:
    def __init__(self, blocks):
        time = lax.axis_index("tm")
        self.blocks = blocks
        self.z, self.q = lax.div(time, STEPS), lax.rem(time, STEPS)
        self.y, self.x = lax.div(self.q, SIDE), lax.rem(self.q, SIDE)
        self.core = lax.axis_index("rows")
        self.partner = {"tm": time, "rows": 1 - self.core}

    def chip(self, dy, dx):
        return lax.rem(self.y + dy % SIDE, SIDE) * SIDE + lax.rem(self.x + dx % SIDE, SIDE)

    def device(self, q, core):
        return {"tm": self.z * STEPS + q, "rows": core}

    def above(self, dz):
        z = lax.rem(self.z + dz % self.blocks, self.blocks)
        return {"tm": z * STEPS + self.q, "rows": self.core}


def remote(src, dst, send, recv, device):
    return pltpu.make_async_remote_copy(
        src_ref=src, dst_ref=dst, send_sem=send, recv_sem=recv, device_id=device, device_id_type=pl.DeviceIdType.MESH
    )


class Gather:
    def __init__(self, place, own, buf, send, recv, side_send, side_recv, local):
        self.place, self.own, self.buf = place, own, buf
        self.half, self.quarter = own.shape[0] // 2, own.shape[0] // 4
        self.sems, self.side_sems = (send, recv), (side_send, side_recv)
        self.keep = pltpu.make_async_copy(own, buf.at[place.q, place.core], local)
        signs, sides = (1, -1), (0, 1)
        keys = [("a1", h, s) for h in sides for s in signs] + [("a2", h, s) for h in sides for s in signs]
        keys += [(name, h, o, s) for name in ("b1", "b2") for h in sides for o in (0, -1, 1, 2) for s in signs]
        self.keys = {key: i for i, key in enumerate(keys)}

    @staticmethod
    def off(h, along, across=0):
        return ((across, along), (along, across))[h]

    def copy(self, key):
        name, h, s = key[0], key[1], key[-1]
        start, size = h * self.half, self.half
        if name == "a1":
            offset, to = (0, 0), self.off(h, s)
        elif name == "a2":
            offset, to = self.off(h, -s), self.off(h, s)
        elif name == "b1":
            offset, to = self.off(h, key[2]), self.off(h, 0, s)
        else:
            offset, to = self.off(h, key[2], -s), self.off(h, 0, s)
        if name in ("a2", "b2"):
            start, size = start + (self.quarter if s < 0 else 0), self.quarter
        place, i = self.place, self.keys[key]
        dst = self.buf.at[place.chip(*offset), place.core, pl.ds(start, size)]
        src = self.own.at[pl.ds(start, size)] if offset == (0, 0) else dst
        return remote(src, dst, self.sems[0].at[i], self.sems[1].at[i], place.device(place.chip(*to), place.core))

    def across(self, h, offset):
        place, dy, dx = self.place, offset[0] % SIDE, offset[1] % SIDE
        i = h * STEPS + dy * SIDE + dx
        part = pl.ds(h * self.half, self.half)
        dst = self.buf.at[place.chip(dy, dx), place.core, part]
        src = self.own.at[part] if (dy, dx) == (0, 0) else dst
        return remote(src, dst, self.side_sems[0].at[i], self.side_sems[1].at[i], place.partner)

    def begin(self):
        for name, rest in (("a1", ()), ("b1", (0,))):
            for h in (0, 1):
                for s in (1, -1):
                    self.copy((name, h, *rest, s)).start()
        for h in (0, 1):
            self.across(h, (0, 0)).start()
        self.keep.start()

    def relay(self, h, o, s):
        self.copy(("b1", h, o, s)).wait_recv()
        self.copy(("b2", h, o, s)).start()
        self.across(h, self.off(h, o, -s)).start()

    def stage(self, number):
        if number == 0:
            for s in (1, -1):
                for h in (0, 1):
                    self.copy(("a1", h, s)).wait_recv()
                    self.copy(("a2", h, s)).start()
                    for t in (1, -1):
                        self.copy(("b1", h, -s, t)).start()
                    self.across(h, self.off(h, -s)).start()
        if number == 1:
            for s in (1, -1):
                for h in (0, 1):
                    self.relay(h, 0, s)
            for h in (0, 1):
                for s in (1, -1):
                    self.copy(("a2", h, s)).wait_recv()
                for t in (1, -1):
                    self.copy(("b1", h, 2, t)).start()
                self.across(h, self.off(h, 2)).start()
        if number in (2, 3):
            for o in ((-1, 1), (2,))[number - 2]:
                for s in (1, -1):
                    for h in (0, 1):
                        self.relay(h, o, s)

    def finish(self):
        for o in (0, -1, 1, 2):
            for h in (0, 1):
                for s in (1, -1):
                    self.copy(("b2", h, o, s)).wait_recv()
                self.across(h, self.off(h, o, 2)).start()
        for i in range(STEPS):
            for h in (0, 1):
                self.across(h, divmod(i, SIDE)).wait()
        self.keep.wait()
        for key in self.keys:
            self.copy(key).wait_send()


class GatherRows:
    def __init__(self, place, own, buf, send, recv, side_send, side_recv, local):
        self.place, self.own, self.buf = place, own, buf
        self.sems, self.side_sems = (send, recv), (side_send, side_recv)
        self.keep = pltpu.make_async_copy(own, buf.at[place.q, place.core], local)
        self.order = sorted(range(1, STEPS), key=lambda i: -sum(min(k, SIDE - k) for k in divmod(i, SIDE)))

    def copy(self, i):
        place, (dy, dx) = self.place, divmod(i, SIDE)
        to = place.device(place.chip(dy, dx), place.core)
        return remote(self.own, self.buf.at[place.q, place.core], self.sems[0].at[i], self.sems[1].at[i], to)

    def across(self, i):
        place, (dy, dx) = self.place, divmod(i, SIDE)
        dst = self.buf.at[place.chip(-dy, -dx), place.core]
        return remote(dst if i else self.own, dst, self.side_sems[0].at[i], self.side_sems[1].at[i], place.partner)

    def begin(self):
        for i in self.order:
            self.copy(i).start()
        self.across(0).start()
        self.keep.start()

    def finish(self):
        for i in reversed(self.order):
            self.copy(i).wait_recv()
            self.across(i).start()
        for i in range(STEPS):
            self.across(i).wait()
        self.keep.wait()
        for i in self.order:
            self.copy(i).wait_send()


def turned(ref, i, start):
    return ref[i, pl.ds(start, LANE, stride=2), :].T


def kernel(blocks, rates, mask, gain_rows, watched, back_hbm, start_hbm, filt_rows, smooth_rows,
           gain, back, mid, back_rows, start_rows, woven, spread, obs, prior, filt, smooth,
           gains, backs, seen, kept, pmap, qmap, stage, enter, leave, turn, far, sout, fsend,
           ksend, krecv, kside_s, kside_r, gsend, grecv, gside_s, gside_r,
           osend, orecv, msend, mrecv, mside_s, mside_r, chain, fsem, ssem, local):
    place = Place(blocks)
    core = place.core
    share = watched.shape[1] // (2 * STEPS)
    paths = watched.shape[1]
    barrier = pltpu.get_barrier_semaphore()
    greet = [place.partner, place.above(1), place.above(-1)]
    for i in range(1, STEPS):
        q = place.chip(*divmod(i, SIDE))
        greet += [place.device(q, core), place.device(q, 1 - core)]
    for device in greet:
        pl.semaphore_signal(barrier, inc=1, device_id=device, device_id_type=pl.DeviceIdType.MESH)
    loads = []
    for i in range(4):
        loads.append(pltpu.make_async_copy(back_hbm.at[:, pl.ds(i * LANE, LANE)], back_rows.at[i], local.at[5 + i]))
    for i in range(paths // LANE):
        loads.append(pltpu.make_async_copy(start_hbm.at[:, pl.ds(i * LANE, LANE)], start_rows.at[i], local.at[9 + i]))
    for load in loads:
        load.start()

    kept_gain = gain_rows[...] * mask[...].astype(F32)
    for i in (0, 1):
        mid[i, pl.ds(0, 2 * LANE), :] = kept_gain[:, i * LANE:(i + 1) * LANE]
        for comp in (0, 1):
            gain[i * LANE:(i + 1) * LANE, comp * LANE:(comp + 1) * LANE] = turned(mid, i, comp)
    pl.semaphore_wait(barrier, len(greet))
    first = Gather(place, gain, gains, ksend, krecv, kside_s, kside_r, local.at[1])
    second = Gather(place, back, backs, gsend, grecv, gside_s, gside_r, local.at[2])
    first.begin()

    sites = watched[...].T
    empty = jnp.zeros((PAD - share, 2 * LANE), F32)
    for i in range(2 * STEPS):
        obs[i // 2, i % 2] = jnp.concatenate([sites[i * share:(i + 1) * share], empty], 0)
    watch = []
    for i in range(1, STEPS):
        q = place.chip(*divmod(i, SIDE))
        copy = remote(obs.at[q, core], seen.at[place.q], osend.at[i], orecv.at[i], place.device(q, core))
        copy.start()
        watch.append(copy)
    own_obs = pltpu.make_async_copy(obs.at[place.q, core], seen.at[place.q], local.at[0])
    own_obs.start()

    for load in loads:
        load.wait()
    live = jnp.where(lax.axis_index("tm") == blocks * STEPS - 1, 0.0, 1.0).astype(F32)
    for comp in (0, 1):
        for i in range(4):
            mid[comp, pl.ds(i * LANE, LANE), :] = turned(back_rows, i, comp) * live
    first.stage(0)
    for block in range(4):
        begin = block // 2 * 2 * LANE + block % 2
        for comp in (0, 1):
            rows = mid[comp, pl.ds(begin, LANE, stride=2), :]
            back[pl.ds(block * LANE, LANE), pl.ds(comp * LANE, LANE)] = rows
    first.stage(1)

    @pl.when(place.z == 0)
    def _():
        row = lax.broadcasted_iota(jnp.int32, (PAD, LANE), 0)
        lane = lax.broadcasted_iota(jnp.int32, (PAD, LANE), 1)
        for block in range(4):
            total = jnp.zeros((PAD, LANE), F32)
            for i in range(paths // LANE):
                wanted = lane + i * LANE == row + (place.q * 2 + core) * share
                pick = jnp.where(jnp.logical_and(wanted, row < share), 1.0, 0.0).astype(BF16)
                rest = start_rows[i, pl.ds(block // 2 * 2 * LANE + block % 2, LANE, stride=2), :]
                for _ in range(3):
                    part = rest.astype(BF16)
                    rest = rest - part.astype(F32)
                    total += lax.dot_general(pick, part, (((1,), (1,)), ((), ())), preferred_element_type=F32)
            prior[:, block * LANE:(block + 1) * LANE] = total

    @pl.when(place.z > 0)
    def _():
        prior[...] = jnp.zeros_like(prior)

    decay = jnp.exp(-rates[...])
    own = (decay * (1.0 + rates[...]), decay * (1.0 - rates[...]))
    other = (decay, -decay * rates[...] * rates[...])

    def ordered(pair):
        return jnp.concatenate([pair[comp][:, half * LANE:(half + 1) * LANE] for half in (0, 1) for comp in (0, 1)], 1)

    alpha, beta = ordered(own), ordered(other)
    first.stage(2)
    first.stage(3)
    second.begin()
    first.finish()
    for copy in watch:
        copy.wait()
    own_obs.wait()

    def moved(state):
        swap = jnp.concatenate([state[:, i * LANE:(i + 1) * LANE] for i in (1, 0, 3, 2)], 1)
        return alpha * state + beta * swap

    def values(state):
        return jnp.concatenate([state[:, :LANE], state[:, 2 * LANE:3 * LANE]], 1)

    row = lax.broadcasted_iota(jnp.int32, (PAD, 4 * LANE), 0)
    lane = lax.broadcasted_iota(jnp.int32, (PAD, 4 * LANE), 1)
    unit = jnp.where(lane == row + (place.q * 2 + core) * PAD, 1.0, 0.0).astype(F32)
    zero = jnp.zeros((PAD, 4 * LANE), F32)
    last = blocks - 1

    def forward(k, state):
        predicted = moved(state)
        target, rows = seen[k], state.shape[0]
        if rows > PAD:
            target = jnp.concatenate([target, jnp.zeros((rows - PAD, 2 * LANE), F32)], 0)
        innovation = target - values(predicted)
        state = predicted + jnp.concatenate([product(innovation, gains[k, half]) for half in (0, 1)], 1)
        kept[k] = state[:PAD]
        return state

    def mapped(state, table):
        return product(state, table[...].reshape(4 * LANE, 4 * LANE))

    both = lax.fori_loop(0, STEPS, forward, jnp.concatenate([prior[...], unit], 0))
    leave[...] = both[:PAD]
    stage[...] = both[PAD:]
    up = remote(leave, enter, chain.at[0], chain.at[1], place.above(1))
    maps = GatherRows(place, stage, pmap, msend.at[0], mrecv.at[0], mside_s.at[0], mside_r.at[0], local.at[3])
    through = jnp.logical_and(place.z >= 2, place.z < last)

    @pl.when(place.z == 0)
    def _():
        up.start()

    @pl.when(through)
    def _():
        maps.begin()

    second.stage(0)

    def filter_again():
        return lax.fori_loop(0, STEPS, forward, enter[...])

    @pl.when(place.z == 1)
    def _():
        up.wait_recv()
        leave[...] = filter_again()
        up.start()

    @pl.when(through)
    def _():
        maps.finish()
    second.stage(1)

    @pl.when(place.z >= last - 1)
    def _():
        second.stage(2)

    @pl.when(place.z >= 2)
    def _():
        up.wait_recv()

    @pl.when(through)
    def _():
        leave[...] = leave[...] + mapped(enter[...], pmap)
        up.start()

    @pl.when(place.z < last - 1)
    def _():
        second.stage(2)

    second.stage(3)

    @pl.when(place.z >= 2)
    def _():
        filter_again()

    @pl.when(place.z < last)
    def _():
        up.wait_send()
    second.finish()

    def back_product(k, value):
        return jnp.concatenate([product(value, backs[k, half]) for half in (0, 1)], 1)

    def keep_smooth(k, state):
        sout[k, 0] = state[:, :2 * LANE]
        sout[k, 1] = state[:, 2 * LANE:]

    def both_back(i, state):
        k = STEPS - 1 - i
        held = kept[k]
        wanted = jnp.concatenate([state[:PAD] - moved(held), state[PAD:]], 0)
        state = jnp.concatenate([held, zero], 0) + back_product(k, wanted)
        keep_smooth(k, state[:PAD])
        return state

    both = lax.fori_loop(0, STEPS, both_back, jnp.concatenate([zero, unit], 0))
    turn[...] = both[PAD:]
    far[0] = both[:PAD]
    turns = GatherRows(place, turn, qmap, msend.at[1], mrecv.at[1], mside_s.at[1], mside_r.at[1], local.at[4])
    down = remote(far.at[0], far.at[1], chain.at[2], chain.at[3], place.above(-1))
    through = jnp.logical_and(place.z >= 1, place.z < last - 1)

    def hand_on(value_ref, k, out, sem):
        for half in (0, 1):
            part = value_ref.at[k, half]
            home = jnp.logical_and(k == place.q, core == half)

            @pl.when(home)
            def _():
                pltpu.make_async_copy(part, out.at[place.q, core], sem.at[1]).start()

            @pl.when(jnp.logical_not(home))
            def _():
                remote(part, out.at[place.q, core], sem.at[0], sem.at[1], place.device(k, half)).start()

    def hand_filtered(k, carry):
        fsend[k, 0] = kept[k, :, pl.ds(0, 2 * LANE)]
        fsend[k, 1] = kept[k, :, pl.ds(2 * LANE, 2 * LANE)]
        hand_on(fsend, k, filt, fsem)
        return carry

    def hand_smoothed(i, carry):
        hand_on(sout, STEPS - 1 - i, smooth, ssem)
        return carry

    def all_handed(out, sem):
        pltpu.make_async_copy(out, out, sem.at[1]).wait()
        rest = out.at[pl.ds(0, STEPS - 1)]
        pltpu.make_async_copy(rest, rest, sem.at[0]).wait()
        pltpu.make_async_copy(out.at[0, 0], out.at[0, 0], sem.at[0]).wait()

    def emit(table, rows):
        for i in range(2 * STEPS):
            spread[pl.ds(i * share, share), :] = table[i // 2, i % 2, pl.ds(0, share), :]
        for comp in (0, 1):
            for i in range(paths // LANE):
                block = spread[pl.ds(i * LANE, LANE), pl.ds(comp * LANE, LANE)]
                woven[i, pl.ds(comp, LANE, stride=2), :] = block.T
        for i in range(paths // LANE):
            rows[:, i * LANE:(i + 1) * LANE] = woven[i]

    def smooth_again():
        def step(i, state):
            k = STEPS - 1 - i
            state = kept[k] + back_product(k, state - moved(kept[k]))
            keep_smooth(k, state)
            hand_on(sout, k, smooth, ssem)
            return state

        return lax.fori_loop(0, STEPS, step, far[1])

    @pl.when(place.z == last)
    def _():
        down.start()

    @pl.when(through)
    def _():
        turns.begin()

    @pl.when(place.z == last - 1)
    def _():
        down.wait_recv()
        far[0] = smooth_again()
        down.start()

    @pl.when(through)
    def _():
        turns.finish()
    lax.fori_loop(0, STEPS, hand_filtered, 0)

    @pl.when(place.z == last)
    def _():
        lax.fori_loop(0, STEPS, hand_smoothed, 0)

    @pl.when(place.z < last // 2)
    def _():
        all_handed(filt, fsem)
        emit(filt, filt_rows)

    @pl.when(place.z < last - 1)
    def _():
        down.wait_recv()

    @pl.when(through)
    def _():
        far[0] = far[0] + mapped(far[1], qmap)
        down.start()

    @pl.when(place.z < last - 1)
    def _():
        smooth_again()

    @pl.when(place.z > 0)
    def _():
        down.wait_send()

    @pl.when(place.z >= last // 2)
    def _():
        all_handed(filt, fsem)
        emit(filt, filt_rows)

    all_handed(smooth, ssem)
    emit(smooth, smooth_rows)


def body(site_rates, prior_mean, observed, obs_mask, filter_gains, smooth_gains):
    blocks = lax.axis_size("tm") // STEPS
    paths = prior_mean.shape[1]
    vmem, dma = pl.BlockSpec(memory_space=pltpu.VMEM), pltpu.SemaphoreType.DMA
    out = jax.ShapeDtypeStruct((2 * LANE, paths), F32)
    shared = (STEPS, 2, PAD, 2 * LANE)
    wide = (STEPS, 2, PAD, 4 * LANE)
    narrow = (PAD, 4 * LANE)
    sizes = [
        (2 * LANE, 2 * LANE), (4 * LANE, 2 * LANE), (2, 4 * LANE, LANE), (4, 2 * LANE, LANE),
        (paths // LANE, 4 * LANE, LANE), (paths // LANE, 2 * LANE, LANE), (paths, 2 * LANE), shared, narrow, shared, shared,
        (STEPS, 2, 2 * LANE, 2 * LANE), (STEPS, 2, 4 * LANE, 2 * LANE), (STEPS, PAD, 2 * LANE), (STEPS, PAD, 4 * LANE),
        wide, wide, narrow, narrow, narrow, narrow, (2, *narrow), shared, shared,
    ]
    filt, smooth = pl.pallas_call(
        functools.partial(kernel, blocks),
        out_shape=(out, out),
        in_specs=[vmem] * 4 + [pl.BlockSpec(memory_space=pl.ANY)] * 2,
        out_specs=(vmem, vmem),
        scratch_shapes=[pltpu.VMEM(size, F32) for size in sizes] + [
            dma((40,)), dma((40,)), dma((32,)), dma((32,)),
            dma((40,)), dma((40,)), dma((32,)), dma((32,)),
            dma((STEPS,)), dma((STEPS,)),
            dma((2, STEPS)), dma((2, STEPS)), dma((2, STEPS)), dma((2, STEPS)),
            dma((4,)), dma((2,)), dma((2,)), dma((12,)),
        ],
        compiler_params=pltpu.CompilerParams(
            collective_id=0, has_side_effects=True, vmem_limit_bytes=60 * 1024 * 1024
        ),
        name="two_level_scan",
    )(site_rates[None], obs_mask, filter_gains[0], observed[0], smooth_gains[0], prior_mean)
    return filt[None], smooth[None]


def solution(mesh):
    placed = (
        P(),
        P(),
        P("tm", None, None),
        P("tm", None),
        P("tm", "rows", None),
        P("tm", "rows", None),
    )
    return jax.shard_map(
        body,
        mesh=mesh,
        in_specs=placed,
        out_specs=(P("tm", "rows", None), P("tm", "rows", None)),
        check_vma=False,
    )
```

time: 576 us -> 142 us (0.25)
  the two profiles are of different devices: /device:TPU:75 before, /device:TPU:1 now
where the time goes in v2:
time: 142 us; the launch traced here: 141 us
  Pallas kernels  138 us (97%)
  local copies, waits for them, and re-layouts  2.57 us (2%)
    pallas_call x1, Pallas kernels, body(): pl.pallas_call(functools.partial(kernel, blocks), out_shape=(out, out), i...  138 us

profile of v2, /device:TPU:1, one launch (start us, length us, event | category | flops | bytes accessed | tf_op | source)
XLA Modules:
  0.0 141.5 jit_solution(3635005719896619769)
XLA Ops:
  0.6 138.3 %two_level_scan.1 = (f32[256,384]{1,0:T(8,128)}, f32[256,384]{1,0:T(8,128)}) custom-call(f32[1,256]{1,0:T(1,128)} %bitcast.11, s32[1,256]{1,0:T(1,128)} %mask.1, f32[256,256]{1,0:T(8,128)} %bitcast.10, f32[256,384]{1,0:T(8,128)} %bitcast.9, f32[256,512]{1,0:T(8,128)} %bitcast.6, f32[512,384]{1,0:T(8,128)} %start_hbm.1), custom_call_target="tpu_custom_call" | custom-call | tf_op jit(solution)/shard_map/two_level_scan/pallas_call | solution.py:510
  138.9 0.0 copy-start
  138.9 1.8 %copy.10 = f32[1,256,384]{2,1,0:T(8,128)} copy(f32[1,256,384]{2,1,0:T(8,128)} %bitcast.8) | data formatting | bytes 786432
  140.7 0.0 copy-done
  140.7 0.7 copy.11
Async XLA Ops:
  138.9 1.8 %copy-start = (f32[256,384]{1,0:T(8,128)S(1)}, f32[256,384]{1,0:T(8,128)}, u32[]{:S(2)}) copy-start(f32[256,384]{1,0:T(8,128)} %get-tuple-element.5) | copy-start | bytes 1179652

commit v3 on v2

--- a/solution.py
+++ b/solution.py
@@ -142,8 +142,13 @@
                 self.across(h, self.off(h, o, 2)).start()
         for i in range(STEPS):
             for h in (0, 1):
-                self.across(h, divmod(i, SIDE)).wait()
+                self.across(h, divmod(i, SIDE)).wait_recv()
         self.keep.wait()
+
+    def drain(self):
+        for i in range(STEPS):
+            for h in (0, 1):
+                self.across(h, divmod(i, SIDE)).wait_send()
         for key in self.keys:
             self.copy(key).wait_send()
 
@@ -176,8 +181,12 @@
             self.copy(i).wait_recv()
             self.across(i).start()
         for i in range(STEPS):
-            self.across(i).wait()
+            self.across(i).wait_recv()
         self.keep.wait()
+
+    def drain(self):
+        for i in range(STEPS):
+            self.across(i).wait_send()
         for i in self.order:
             self.copy(i).wait_send()
 
@@ -188,7 +197,7 @@
 
 def kernel(blocks, rates, mask, gain_rows, watched, back_hbm, start_hbm, filt_rows, smooth_rows,
            gain, back, mid, back_rows, start_rows, woven, spread, obs, prior, filt, smooth,
-           gains, backs, seen, kept, pmap, qmap, stage, enter, leave, turn, far, sout, fsend,
+           gains, backs, seen, kept, pmap, qmap, parts, stage, enter, leave, turn, far, near, sout, fsend,
            ksend, krecv, kside_s, kside_r, gsend, grecv, gside_s, gside_r,
            osend, orecv, msend, mrecv, mside_s, mside_r, chain, fsem, ssem, local):
     place = Place(blocks)
@@ -220,19 +229,6 @@
     second = Gather(place, back, backs, gsend, grecv, gside_s, gside_r, local.at[2])
     first.begin()
 
-    sites = watched[...].T
-    empty = jnp.zeros((PAD - share, 2 * LANE), F32)
-    for i in range(2 * STEPS):
-        obs[i // 2, i % 2] = jnp.concatenate([sites[i * share:(i + 1) * share], empty], 0)
-    watch = []
-    for i in range(1, STEPS):
-        q = place.chip(*divmod(i, SIDE))
-        copy = remote(obs.at[q, core], seen.at[place.q], osend.at[i], orecv.at[i], place.device(q, core))
-        copy.start()
-        watch.append(copy)
-    own_obs = pltpu.make_async_copy(obs.at[place.q, core], seen.at[place.q], local.at[0])
-    own_obs.start()
-
     for load in loads:
         load.wait()
     live = jnp.where(lax.axis_index("tm") == blocks * STEPS - 1, 0.0, 1.0).astype(F32)
@@ -247,6 +243,18 @@
             back[pl.ds(block * LANE, LANE), pl.ds(comp * LANE, LANE)] = rows
     first.stage(1)
 
+    sites = watched[...].T
+    for i in range(2 * STEPS):
+        obs[i // 2, i % 2] = sites[i * share:(i + 1) * share]
+    watch = []
+    for i in range(1, STEPS):
+        q = place.chip(*divmod(i, SIDE))
+        copy = remote(obs.at[q, core], seen.at[place.q], osend.at[i], orecv.at[i], place.device(q, core))
+        copy.start()
+        watch.append(copy)
+    own_obs = pltpu.make_async_copy(obs.at[place.q, core], seen.at[place.q], local.at[0])
+    own_obs.start()
+
     @pl.when(place.z == 0)
     def _():
         row = lax.broadcasted_iota(jnp.int32, (PAD, LANE), 0)
@@ -280,7 +288,7 @@
     second.begin()
     first.finish()
     for copy in watch:
-        copy.wait()
+        copy.wait_recv()
     own_obs.wait()
 
     def moved(state):
@@ -298,27 +306,57 @@
 
     def forward(k, state):
         predicted = moved(state)
-        target, rows = seen[k], state.shape[0]
-        if rows > PAD:
-            target = jnp.concatenate([target, jnp.zeros((rows - PAD, 2 * LANE), F32)], 0)
+        target = jnp.concatenate([seen[k], jnp.zeros((state.shape[0] - share, 2 * LANE), F32)], 0)
         innovation = target - values(predicted)
         state = predicted + jnp.concatenate([product(innovation, gains[k, half]) for half in (0, 1)], 1)
         kept[k] = state[:PAD]
         return state
 
-    def mapped(state, table):
-        return product(state, table[...].reshape(4 * LANE, 4 * LANE))
+    def whole(ref):
+        state = jnp.concatenate([ref[0], ref[1]], 1)
+        return jnp.concatenate([state, jnp.zeros((PAD - share, 4 * LANE), F32)], 0)
+
+    def put(ref, state):
+        for half in (0, 1):
+            ref[half] = state[:share, half * 2 * LANE:(half + 1) * 2 * LANE]
+
+    def parts_of(table):
+        for q in range(STEPS):
+            for i in (0, 1):
+                high, low = halves(table[q, i])
+                rows = pl.ds((q * 2 + i) * PAD, PAD)
+                parts[0, rows, :] = high
+                parts[1, rows, :] = low
+
+    def hop(link, given, offset):
+        dot = functools.partial(jnp.dot, preferred_element_type=F32)
+        pair = []
+        for half in (0, 1):
+            link[half].wait_recv()
+            value = jnp.concatenate([given[half], jnp.zeros((PAD - share, 2 * LANE), F32)], 0)
+            high, low = halves(value)
+            pair.append((high, jnp.concatenate([high, low], 0)))
+        for half in (0, 1):
+            lanes = pl.ds(half * 2 * LANE, 2 * LANE)
+            total = offset[half]
+            for part in (0, 1):
+                rows = pl.ds(part * 2 * LANE, 2 * LANE)
+                both = dot(pair[part][1], parts[0, rows, lanes])
+                total += (both[:PAD] + (both[PAD:] + dot(pair[part][0], parts[1, rows, lanes])))[:share]
+            offset[half] = total
+            link[half].start()
 
     both = lax.fori_loop(0, STEPS, forward, jnp.concatenate([prior[...], unit], 0))
-    leave[...] = both[:PAD]
+    put(leave, both)
     stage[...] = both[PAD:]
-    up = remote(leave, enter, chain.at[0], chain.at[1], place.above(1))
+    up = [remote(leave.at[i], enter.at[i], chain.at[0, i], chain.at[1, i], place.above(1)) for i in (0, 1)]
     maps = GatherRows(place, stage, pmap, msend.at[0], mrecv.at[0], mside_s.at[0], mside_r.at[0], local.at[3])
     through = jnp.logical_and(place.z >= 2, place.z < last)
 
     @pl.when(place.z == 0)
     def _():
-        up.start()
+        for copy in up:
+            copy.start()
 
     @pl.when(through)
     def _():
@@ -327,53 +365,52 @@
     second.stage(0)
 
     def filter_again():
-        return lax.fori_loop(0, STEPS, forward, enter[...])
+        return lax.fori_loop(0, STEPS, forward, whole(enter))
 
     @pl.when(place.z == 1)
     def _():
-        up.wait_recv()
-        leave[...] = filter_again()
-        up.start()
+        for copy in up:
+            copy.wait_recv()
+        put(leave, filter_again())
+        for copy in up:
+            copy.start()
 
     @pl.when(through)
     def _():
         maps.finish()
+        parts_of(pmap)
     second.stage(1)
 
     @pl.when(place.z >= last - 1)
     def _():
         second.stage(2)
 
+    @pl.when(place.z == last)
+    def _():
+        for copy in up:
+            copy.wait_recv()
+
+    @pl.when(through)
+    def _():
+        hop(up, enter, leave)
+
+    @pl.when(place.z < last - 1)
+    def _():
+        second.stage(2)
+
+    second.stage(3)
+
     @pl.when(place.z >= 2)
     def _():
-        up.wait_recv()
-
-    @pl.when(through)
-    def _():
-        leave[...] = leave[...] + mapped(enter[...], pmap)
-        up.start()
-
-    @pl.when(place.z < last - 1)
-    def _():
-        second.stage(2)
-
-    second.stage(3)
-
-    @pl.when(place.z >= 2)
-    def _():
         filter_again()
 
-    @pl.when(place.z < last)
-    def _():
-        up.wait_send()
     second.finish()
 
     def back_product(k, value):
         return jnp.concatenate([product(value, backs[k, half]) for half in (0, 1)], 1)
 
     def keep_smooth(k, state):
-        sout[k, 0] = state[:, :2 * LANE]
-        sout[k, 1] = state[:, 2 * LANE:]
+        put(sout.at[k], state)
 
     def both_back(i, state):
         k = STEPS - 1 - i
@@ -385,9 +422,9 @@
 
     both = lax.fori_loop(0, STEPS, both_back, jnp.concatenate([zero, unit], 0))
     turn[...] = both[PAD:]
-    far[0] = both[:PAD]
+    put(far, both)
     turns = GatherRows(place, turn, qmap, msend.at[1], mrecv.at[1], mside_s.at[1], mside_r.at[1], local.at[4])
-    down = remote(far.at[0], far.at[1], chain.at[2], chain.at[3], place.above(-1))
+    down = [remote(far.at[i], near.at[i], chain.at[2, i], chain.at[3, i], place.above(-1)) for i in (0, 1)]
     through = jnp.logical_and(place.z >= 1, place.z < last - 1)
 
     def hand_on(value_ref, k, out, sem):
@@ -404,8 +441,7 @@
                 remote(part, out.at[place.q, core], sem.at[0], sem.at[1], place.device(k, half)).start()
 
     def hand_filtered(k, carry):
-        fsend[k, 0] = kept[k, :, pl.ds(0, 2 * LANE)]
-        fsend[k, 1] = kept[k, :, pl.ds(2 * LANE, 2 * LANE)]
+        put(fsend.at[k], kept[k])
         hand_on(fsend, k, filt, fsem)
         return carry
 
@@ -421,7 +457,7 @@
 
     def emit(table, rows):
         for i in range(2 * STEPS):
-            spread[pl.ds(i * share, share), :] = table[i // 2, i % 2, pl.ds(0, share), :]
+            spread[pl.ds(i * share, share), :] = table[i // 2, i % 2]
         for comp in (0, 1):
             for i in range(paths // LANE):
                 block = spread[pl.ds(i * LANE, LANE), pl.ds(comp * LANE, LANE)]
@@ -437,11 +473,12 @@
             hand_on(sout, k, smooth, ssem)
             return state
 
-        return lax.fori_loop(0, STEPS, step, far[1])
+        return lax.fori_loop(0, STEPS, step, whole(near))
 
     @pl.when(place.z == last)
     def _():
-        down.start()
+        for copy in down:
+            copy.start()
 
     @pl.when(through)
     def _():
@@ -449,46 +486,79 @@
 
     @pl.when(place.z == last - 1)
     def _():
-        down.wait_recv()
-        far[0] = smooth_again()
-        down.start()
+        for copy in down:
+            copy.wait_recv()
+        put(far, smooth_again())
+        for copy in down:
+            copy.start()
 
     @pl.when(through)
     def _():
         turns.finish()
-    lax.fori_loop(0, STEPS, hand_filtered, 0)
-
-    @pl.when(place.z == last)
-    def _():
-        lax.fori_loop(0, STEPS, hand_smoothed, 0)
+        parts_of(qmap)
+
+    def hand_all_filtered():
+        lax.fori_loop(0, STEPS, hand_filtered, 0)
+
+    early = place.z < last // 2 + 1
+
+    @pl.when(early)
+    def _():
+        hand_all_filtered()
 
     @pl.when(place.z < last // 2)
     def _():
         all_handed(filt, fsem)
         emit(filt, filt_rows)
 
+    @pl.when(place.z == 0)
+    def _():
+        for copy in down:
+            copy.wait_recv()
+
+    @pl.when(through)
+    def _():
+        hop(down, near, far)
+
+    @pl.when(jnp.logical_not(early))
+    def _():
+        hand_all_filtered()
+
+    @pl.when(place.z == last)
+    def _():
+        lax.fori_loop(0, STEPS, hand_smoothed, 0)
+
     @pl.when(place.z < last - 1)
     def _():
-        down.wait_recv()
-
-    @pl.when(through)
-    def _():
-        far[0] = far[0] + mapped(far[1], qmap)
-        down.start()
-
-    @pl.when(place.z < last - 1)
-    def _():
         smooth_again()
-
-    @pl.when(place.z > 0)
-    def _():
-        down.wait_send()
 
     @pl.when(place.z >= last // 2)
     def _():
         all_handed(filt, fsem)
         emit(filt, filt_rows)
 
+    @pl.when(place.z < last)
+    def _():
+        for copy in up:
+            copy.wait_send()
+
+    @pl.when(place.z > 0)
+    def _():
+        for copy in down:
+            copy.wait_send()
+
+    @pl.when(jnp.logical_and(place.z >= 2, place.z < last))
+    def _():
+        maps.drain()
+
+    @pl.when(through)
+    def _():
+        turns.drain()
+
+    first.drain()
+    second.drain()
+    for copy in watch:
+        copy.wait_send()
     all_handed(smooth, ssem)
     emit(smooth, smooth_rows)
 
@@ -498,26 +568,27 @@
     paths = prior_mean.shape[1]
     vmem, dma = pl.BlockSpec(memory_space=pltpu.VMEM), pltpu.SemaphoreType.DMA
     out = jax.ShapeDtypeStruct((2 * LANE, paths), F32)
-    shared = (STEPS, 2, PAD, 2 * LANE)
+    share = paths // (2 * STEPS)
+    shared, chained = (STEPS, 2, share, 2 * LANE), (2, share, 2 * LANE)
     wide = (STEPS, 2, PAD, 4 * LANE)
     narrow = (PAD, 4 * LANE)
     sizes = [
         (2 * LANE, 2 * LANE), (4 * LANE, 2 * LANE), (2, 4 * LANE, LANE), (4, 2 * LANE, LANE),
         (paths // LANE, 4 * LANE, LANE), (paths // LANE, 2 * LANE, LANE), (paths, 2 * LANE), shared, narrow, shared, shared,
-        (STEPS, 2, 2 * LANE, 2 * LANE), (STEPS, 2, 4 * LANE, 2 * LANE), (STEPS, PAD, 2 * LANE), (STEPS, PAD, 4 * LANE),
-        wide, wide, narrow, narrow, narrow, narrow, (2, *narrow), shared, shared,
+        (STEPS, 2, 2 * LANE, 2 * LANE), (STEPS, 2, 4 * LANE, 2 * LANE), (STEPS, share, 2 * LANE), (STEPS, PAD, 4 * LANE),
+        wide, wide, (BF16, 2, 4 * LANE, 4 * LANE), narrow, chained, chained, narrow, chained, chained, shared, shared,
     ]
     filt, smooth = pl.pallas_call(
         functools.partial(kernel, blocks),
         out_shape=(out, out),
         in_specs=[vmem] * 4 + [pl.BlockSpec(memory_space=pl.ANY)] * 2,
         out_specs=(vmem, vmem),
-        scratch_shapes=[pltpu.VMEM(size, F32) for size in sizes] + [
+        scratch_shapes=[pltpu.VMEM(size[-3:], BF16) if size[0] is BF16 else pltpu.VMEM(size, F32) for size in sizes] + [
             dma((40,)), dma((40,)), dma((32,)), dma((32,)),
             dma((40,)), dma((40,)), dma((32,)), dma((32,)),
             dma((STEPS,)), dma((STEPS,)),
             dma((2, STEPS)), dma((2, STEPS)), dma((2, STEPS)), dma((2, STEPS)),
-            dma((4,)), dma((2,)), dma((2,)), dma((12,)),
+            dma((4, 2)), dma((2,)), dma((2,)), dma((12,)),
         ],
         compiler_params=pltpu.CompilerParams(
             collective_id=0, has_side_effects=True, vmem_limit_bytes=60 * 1024 * 1024

time: 142 us -> 139 us (0.979)
  Pallas kernels: 138 us -> 136 us
    pallas_call x1, Pallas kernels: 138 us -> 136 us  [body(): pl.pallas_call(functools.partial(kernel, blocks), out_shape=(out, out), i...]
where the time goes in v3:
time: 139 us
  Pallas kernels  136 us (98%)
  local copies, waits for them, and re-layouts  2.57 us (2%)
    pallas_call x1, Pallas kernels, body(): pl.pallas_call(functools.partial(kernel, blocks), out_shape=(out, out), i...  136 us

profile of v3, /device:TPU:1, one launch (start us, length us, event | category | flops | bytes accessed | tf_op | source)
XLA Modules:
  0.0 139.1 jit_solution(9774931370218665414)
XLA Ops:
  0.6 135.9 %two_level_scan.1 = (f32[256,384]{1,0:T(8,128)}, f32[256,384]{1,0:T(8,128)}) custom-call(f32[1,256]{1,0:T(1,128)} %bitcast.11, s32[1,256]{1,0:T(1,128)} %mask.1, f32[256,256]{1,0:T(8,128)} %bitcast.10, f32[256,384]{1,0:T(8,128)} %bitcast.9, f32[256,512]{1,0:T(8,128)} %bitcast.6, f32[512,384]{1,0:T(8,128)} %start_hbm.1), custom_call_target="tpu_custom_call" | custom-call | tf_op jit(solution)/shard_map/two_level_scan/pallas_call | solution.py:581
  136.5 0.0 copy-start
  136.5 1.8 %copy.10 = f32[1,256,384]{2,1,0:T(8,128)} copy(f32[1,256,384]{2,1,0:T(8,128)} %bitcast.8) | data formatting | bytes 786432
  138.3 0.0 copy-done
  138.3 0.7 copy.11
Async XLA Ops:
  136.5 1.8 %copy-start = (f32[256,384]{1,0:T(8,128)S(1)}, f32[256,384]{1,0:T(8,128)}, u32[]{:S(2)}) copy-start(f32[256,384]{1,0:T(8,128)} %get-tuple-element.5) | copy-start | bytes 1179652

commit v4 on v3

--- a/solution.py
+++ b/solution.py
@@ -11,6 +11,7 @@
 SIDE = 4
 STEPS = SIDE * SIDE
 LANE = 128
+DIRECT = 5
 PAD = 16
 
 
@@ -115,31 +116,35 @@
                 for h in (0, 1):
                     self.copy(("a1", h, s)).wait_recv()
                     self.copy(("a2", h, s)).start()
+            for s in (1, -1):
+                for h in (0, 1):
                     for t in (1, -1):
                         self.copy(("b1", h, -s, t)).start()
                     self.across(h, self.off(h, -s)).start()
         if number == 1:
-            for s in (1, -1):
-                for h in (0, 1):
-                    self.relay(h, 0, s)
             for h in (0, 1):
                 for s in (1, -1):
                     self.copy(("a2", h, s)).wait_recv()
                 for t in (1, -1):
                     self.copy(("b1", h, 2, t)).start()
                 self.across(h, self.off(h, 2)).start()
+            for s in (1, -1):
+                for h in (0, 1):
+                    self.relay(h, 0, s)
         if number in (2, 3):
             for o in ((-1, 1), (2,))[number - 2]:
                 for s in (1, -1):
                     for h in (0, 1):
                         self.relay(h, o, s)
 
-    def finish(self):
+    def share_last(self):
         for o in (0, -1, 1, 2):
             for h in (0, 1):
                 for s in (1, -1):
                     self.copy(("b2", h, o, s)).wait_recv()
                 self.across(h, self.off(h, o, 2)).start()
+
+    def finish(self):
         for i in range(STEPS):
             for h in (0, 1):
                 self.across(h, divmod(i, SIDE)).wait_recv()
@@ -286,6 +291,7 @@
     first.stage(2)
     first.stage(3)
     second.begin()
+    first.share_last()
     first.finish()
     for copy in watch:
         copy.wait_recv()
@@ -351,7 +357,7 @@
     stage[...] = both[PAD:]
     up = [remote(leave.at[i], enter.at[i], chain.at[0, i], chain.at[1, i], place.above(1)) for i in (0, 1)]
     maps = GatherRows(place, stage, pmap, msend.at[0], mrecv.at[0], mside_s.at[0], mside_r.at[0], local.at[3])
-    through = jnp.logical_and(place.z >= 2, place.z < last)
+    through = jnp.logical_and(place.z > DIRECT, place.z < last)
 
     @pl.when(place.z == 0)
     def _():
@@ -367,41 +373,49 @@
     def filter_again():
         return lax.fori_loop(0, STEPS, forward, whole(enter))
 
-    @pl.when(place.z == 1)
-    def _():
+    def entered():
         for copy in up:
             copy.wait_recv()
+
+    def pass_on():
+        entered()
         put(leave, filter_again())
         for copy in up:
             copy.start()
 
+    @pl.when(jnp.logical_and(place.z > 0, place.z <= 2))
+    def _():
+        pass_on()
+
     @pl.when(through)
     def _():
         maps.finish()
         parts_of(pmap)
+
     second.stage(1)
 
-    @pl.when(place.z >= last - 1)
-    def _():
-        second.stage(2)
+    @pl.when(jnp.logical_or(place.z == 3, place.z == 4))
+    def _():
+        pass_on()
+
+    second.stage(2)
+
+    @pl.when(jnp.logical_and(place.z > 4, place.z <= DIRECT))
+    def _():
+        pass_on()
+
+    second.stage(3)
+
+    @pl.when(through)
+    def _():
+        hop(up, enter, leave)
+        filter_again()
+
+    second.share_last()
 
     @pl.when(place.z == last)
     def _():
-        for copy in up:
-            copy.wait_recv()
-
-    @pl.when(through)
-    def _():
-        hop(up, enter, leave)
-
-    @pl.when(place.z < last - 1)
-    def _():
-        second.stage(2)
-
-    second.stage(3)
-
-    @pl.when(place.z >= 2)
-    def _():
+        entered()
         filter_again()
 
     second.finish()
@@ -420,9 +434,12 @@
         keep_smooth(k, state[:PAD])
         return state
 
-    both = lax.fori_loop(0, STEPS, both_back, jnp.concatenate([zero, unit], 0))
-    turn[...] = both[PAD:]
-    put(far, both)
+    @pl.when(jnp.logical_and(place.z > 0, place.z != last - 1))
+    def _():
+        both = lax.fori_loop(0, STEPS, both_back, jnp.concatenate([zero, unit], 0))
+        turn[...] = both[PAD:]
+        put(far, both)
+
     turns = GatherRows(place, turn, qmap, msend.at[1], mrecv.at[1], mside_s.at[1], mside_r.at[1], local.at[4])
     down = [remote(far.at[i], near.at[i], chain.at[2, i], chain.at[3, i], place.above(-1)) for i in (0, 1)]
     through = jnp.logical_and(place.z >= 1, place.z < last - 1)
@@ -547,7 +564,7 @@
         for copy in down:
             copy.wait_send()
 
-    @pl.when(jnp.logical_and(place.z >= 2, place.z < last))
+    @pl.when(jnp.logical_and(place.z > DIRECT, place.z < last))
     def _():
         maps.drain()
 

time: 139 us -> 134 us (0.964)
  Pallas kernels: 136 us -> 131 us
    pallas_call x1, Pallas kernels: 136 us -> 131 us  [body(): pl.pallas_call(functools.partial(kernel, blocks), out_shape=(out, out), i...]
where the time goes in v4:
time: 134 us
  Pallas kernels  131 us (98%)
  local copies, waits for them, and re-layouts  2.57 us (2%)
    pallas_call x1, Pallas kernels, body(): pl.pallas_call(functools.partial(kernel, blocks), out_shape=(out, out), i...  131 us

profile of v4, /device:TPU:1, one launch (start us, length us, event | category | flops | bytes accessed | tf_op | source)
XLA Modules:
  0.0 133.8 jit_solution(5445354961312562850)
XLA Ops:
  0.6 130.6 %two_level_scan.1 = (f32[256,384]{1,0:T(8,128)}, f32[256,384]{1,0:T(8,128)}) custom-call(f32[1,256]{1,0:T(1,128)} %bitcast.11, s32[1,256]{1,0:T(1,128)} %mask.1, f32[256,256]{1,0:T(8,128)} %bitcast.10, f32[256,384]{1,0:T(8,128)} %bitcast.9, f32[256,512]{1,0:T(8,128)} %bitcast.6, f32[512,384]{1,0:T(8,128)} %start_hbm.1), custom_call_target="tpu_custom_call" | custom-call | tf_op jit(solution)/shard_map/two_level_scan/pallas_call | solution.py:598
  131.3 0.0 copy-start
  131.3 1.8 %copy.10 = f32[1,256,384]{2,1,0:T(8,128)} copy(f32[1,256,384]{2,1,0:T(8,128)} %bitcast.8) | data formatting | bytes 786432
  133.1 0.0 copy-done
  133.1 0.7 copy.11
Async XLA Ops:
  131.3 1.8 %copy-start = (f32[256,384]{1,0:T(8,128)S(1)}, f32[256,384]{1,0:T(8,128)}, u32[]{:S(2)}) copy-start(f32[256,384]{1,0:T(8,128)} %get-tuple-element.5) | copy-start | bytes 1179652

commit v5 on v4

--- a/solution.py
+++ b/solution.py
@@ -336,21 +336,20 @@
 
     def hop(link, given, offset):
         dot = functools.partial(jnp.dot, preferred_element_type=F32)
-        pair = []
-        for half in (0, 1):
-            link[half].wait_recv()
-            value = jnp.concatenate([given[half], jnp.zeros((PAD - share, 2 * LANE), F32)], 0)
+        totals = [offset[0], offset[1]]
+        for part in (0, 1):
+            link[part].wait_recv()
+            value = jnp.concatenate([given[part], jnp.zeros((PAD - share, 2 * LANE), F32)], 0)
             high, low = halves(value)
-            pair.append((high, jnp.concatenate([high, low], 0)))
-        for half in (0, 1):
-            lanes = pl.ds(half * 2 * LANE, 2 * LANE)
-            total = offset[half]
-            for part in (0, 1):
-                rows = pl.ds(part * 2 * LANE, 2 * LANE)
-                both = dot(pair[part][1], parts[0, rows, lanes])
-                total += (both[:PAD] + (both[PAD:] + dot(pair[part][0], parts[1, rows, lanes])))[:share]
-            offset[half] = total
-            link[half].start()
+            stacked = jnp.concatenate([high, low], 0)
+            rows = pl.ds(part * 2 * LANE, 2 * LANE)
+            for half in (0, 1):
+                lanes = pl.ds(half * 2 * LANE, 2 * LANE)
+                both = dot(stacked, parts[0, rows, lanes])
+                totals[half] += (both[:PAD] + (both[PAD:] + dot(high, parts[1, rows, lanes])))[:share]
+                if part:
+                    offset[half] = totals[half]
+                    link[half].start()
 
     both = lax.fori_loop(0, STEPS, forward, jnp.concatenate([prior[...], unit], 0))
     put(leave, both)

time: 134 us -> 133 us (level)
  no operation moved by 1% of the time
where the time goes in v5:
time: 133 us
  Pallas kernels  130 us (98%)
  local copies, waits for them, and re-layouts  2.57 us (2%)
    pallas_call x1, Pallas kernels, body(): pl.pallas_call(functools.partial(kernel, blocks), out_shape=(out, out), i...  130 us

profile of v5, /device:TPU:1, one launch (start us, length us, event | category | flops | bytes accessed | tf_op | source)
XLA Modules:
  0.0 133.2 jit_solution(13022081702998418698)
XLA Ops:
  0.6 129.9 %two_level_scan.1 = (f32[256,384]{1,0:T(8,128)}, f32[256,384]{1,0:T(8,128)}) custom-call(f32[1,256]{1,0:T(1,128)} %bitcast.11, s32[1,256]{1,0:T(1,128)} %mask.1, f32[256,256]{1,0:T(8,128)} %bitcast.10, f32[256,384]{1,0:T(8,128)} %bitcast.9, f32[256,512]{1,0:T(8,128)} %bitcast.6, f32[512,384]{1,0:T(8,128)} %start_hbm.1), custom_call_target="tpu_custom_call" | custom-call | tf_op jit(solution)/shard_map/two_level_scan/pallas_call | solution.py:597
  130.6 0.0 copy-start
  130.6 1.8 %copy.10 = f32[1,256,384]{2,1,0:T(8,128)} copy(f32[1,256,384]{2,1,0:T(8,128)} %bitcast.8) | data formatting | bytes 786432
  132.4 0.0 copy-done
  132.4 0.7 copy.11
Async XLA Ops:
  130.6 1.8 %copy-start = (f32[256,384]{1,0:T(8,128)S(1)}, f32[256,384]{1,0:T(8,128)}, u32[]{:S(2)}) copy-start(f32[256,384]{1,0:T(8,128)} %get-tuple-element.5) | copy-start | bytes 1179652
